TPU v7x, 256 devices: a whole 4x4x8 slice. The times are simulated.
256 devices in a mesh: doc: 64 (over x, z, core), feat: 4 (over y).
Axes of the slice: x: 4, y: 4, z: 8, core: 2. Of those that a mesh axis runs over, the one named last changes fastest.
Arguments:
- b_tiles: bfloat16 [12288, 512, 128], P('doc', 'feat'), may hold values from -0.0625 to 0.0625
- b_rows: int32 [12288, 4], P('doc', 'feat'), may hold values from 0 to 11, as said below
- b_cols: int32 [12288, 4], P('doc', 'feat'), may hold values from 0 to 4095
- b_count: int32 [64, 4], P('doc', 'feat'), may hold values from 144 to 192
- b_offsets: int32 [65], replicated, may hold values from 0 to 480, as said below
- a_tiles: bfloat16 [4096, 512, 128], P('doc', 'feat'), may hold values from -0.375 to 0.375
- a_rows: int32 [4096, 4], P('doc', 'feat'), may hold values from 0 to 12, as said below
- a_tags: int32 [4096, 4], P('doc', 'feat'), may hold values from 0 to 8191, as said below
- a_count: int32 [64, 4], P('doc', 'feat'), may hold values from 48 to 64
- a_offsets: int32 [65], replicated, may hold values from 0 to 480, as said below
- omega_seed: int32 [1], replicated, may hold values from 0 to 1073741823
Outputs:
- tag_sketch: float32 [1048576, 256], P(('doc', 'feat'))
Inputs may be any that keep to these rules, and one draw needn't show every extreme that they name: b_offsets[0] is 0 and each device's range of the text view holds 3 to 12 row blocks. a_offsets[0] is 0 and a_offsets[64] equals b_offsets[64]; every other entry lies 1 to 2 row blocks below the same entry of b_offsets; each device's range of the tag view holds at most 13 row blocks. `b_rows`: below the number of row blocks of the device's range of the text view. `a_rows`: below the number of row blocks of the device's range of the tag view. `a_tags`: the rows of a tile's tag block lie, under the output's placement, on a device with the same feat index as the tile; on one device at most 2 tiles in use have tag blocks on devices of one doc index, and in every draw some doc index gets exactly 2 tiles in use from every device.
All inputs are finite; a program needn't handle non-finite values.
Results may differ from a plain program's by a relative error of at most 0.004.
Values may be sent and summed in bfloat16 or wider, within the bound.
A program may use at most 128 MiB of HBM per device.

v0:
```python
import jax
import jax.numpy as jnp
from jax import lax
from jax.sharding import PartitionSpec as P

TILE = 128
SKETCH = 256
TERMS = 2097152
TAG_DEV = 4096
ROWB_MAX = 12
MARGIN = 2
ROWA_MAX = 13


def passed_along(block, axis, distance):
    devices = range(lax.axis_size(axis))
    route = [(i - distance, i) for i in devices if i - distance in devices]
    return lax.ppermute(block, axis, route)


def unsigned_shift(value, count):
    return lax.shift_right_logical(value, jnp.full(value.shape, count, jnp.int32))


def omega_panel(term_blocks, seed_value):
    row_iota = lax.broadcasted_iota(jnp.int32, (1, TILE, SKETCH), 1)
    col_iota = lax.broadcasted_iota(jnp.int32, (1, TILE, SKETCH), 2)
    mixing = (term_blocks[:, None, None] * TILE + row_iota) * SKETCH + col_iota
    mixing = mixing ^ seed_value * 747796405
    mixing = mixing ^ unsigned_shift(mixing, 16)
    mixing = mixing * 2146121005
    mixing = mixing ^ unsigned_shift(mixing, 15)
    mixing = mixing * -2073254261
    mixing = mixing ^ unsigned_shift(mixing, 16)
    levels = (unsigned_shift(mixing, 8) & 65535).astype(jnp.float32)
    return ((levels - 32767.5) * (3.4641016 / 65536.0)).astype(jnp.bfloat16)


def local(
    b_tiles,
    b_rows,
    b_cols,
    b_count,
    b_offsets,
    a_tiles,
    a_rows,
    a_tags,
    a_count,
    a_offsets,
    omega_seed,
):
    doc_count = lax.axis_size("doc")
    feat_count = lax.axis_size("feat")
    doc_here = lax.axis_index("doc")
    feat_here = lax.axis_index("feat")
    tiles_b = b_tiles.shape[0]
    tiles_a = a_tiles.shape[0]
    highest = lax.Precision.HIGHEST
    slab_blocks = TERMS // (TILE * feat_count)
    panels = omega_panel(b_cols[:, 0] + feat_here * slab_blocks, omega_seed[0])
    tile_terms = jnp.einsum("tij,tjk->tik", b_tiles, panels, preferred_element_type=jnp.float32)
    live_b = jnp.arange(tiles_b, dtype=jnp.int32) < b_count[0, 0]
    chosen = (b_rows[:, 0][None, :] == jnp.arange(ROWB_MAX, dtype=jnp.int32)[:, None]) & live_b[
        None, :
    ]
    partial_value = jnp.einsum(
        "rt,tik->rik", chosen.astype(jnp.float32), tile_terms, precision=highest
    )
    b_start = b_offsets[doc_here]
    b_length = b_offsets[doc_here + 1] - b_start
    shift_rows = a_offsets[doc_here] - b_start + MARGIN
    own_rows = lax.psum(partial_value, "feat").astype(jnp.bfloat16)
    last_rows = lax.dynamic_slice_in_dim(own_rows, b_length - MARGIN, MARGIN, 0)
    arrived = passed_along(last_rows, "doc", 1)
    source = jnp.concatenate([arrived, own_rows], axis=0)
    row_picks = jnp.clip(
        jnp.arange(ROWA_MAX, dtype=jnp.int32) + shift_rows, 0, MARGIN + ROWB_MAX - 1
    )
    z_rows = jnp.take(source, row_picks, axis=0)
    live_a = jnp.arange(tiles_a, dtype=jnp.int32) < a_count[0, 0]
    tile_rows = jnp.take(z_rows, a_rows[:, 0], axis=0)
    tag_blocks = a_tags[:, 0]
    owned_blocks = TAG_DEV // TILE
    capacity = max(2, (tiles_a + doc_count - 1) // doc_count)
    owner_doc = tag_blocks // owned_blocks // feat_count
    owner_hits = (
        (owner_doc[:, None] == jnp.arange(doc_count, dtype=jnp.int32)[None, :]) & live_a[:, None]
    ).astype(jnp.int32)
    earlier = jnp.cumsum(owner_hits, axis=0) - owner_hits
    ranking = jnp.sum(earlier * owner_hits, axis=1)
    slot_index = jnp.where(live_a, owner_doc * capacity + ranking, doc_count * capacity)
    sent_ids = (
        jnp.full((doc_count * capacity,), -1, jnp.int32)
        .at[slot_index]
        .set(tag_blocks, mode="drop")
        .reshape(doc_count, capacity)
    )
    products = jnp.einsum("tij,tik->tjk", a_tiles, tile_rows, preferred_element_type=jnp.float32)
    outbox = (
        jnp.zeros((doc_count * capacity, TILE, SKETCH), jnp.float32)
        .at[slot_index]
        .set(products, mode="drop")
    )
    arrived_sums, arrived_ids = (
        lax.all_to_all(
            outbox.reshape(doc_count, capacity, TILE, SKETCH),
            "doc",
            split_axis=0,
            concat_axis=0,
            tiled=True,
        ),
        lax.all_to_all(sent_ids, "doc", split_axis=0, concat_axis=0, tiled=True),
    )
    flat_here = doc_here * feat_count + feat_here
    local_blocks = arrived_ids.reshape(-1) - flat_here * owned_blocks
    block_pick = (
        jnp.arange(owned_blocks, dtype=jnp.int32)[:, None] == local_blocks[None, :]
    ).astype(jnp.float32)
    sketch = jnp.einsum(
        "bs,sjk->bjk", block_pick, arrived_sums.reshape(-1, TILE, SKETCH), precision=highest
    )
    return sketch.reshape(TAG_DEV, SKETCH)


def solution(mesh):
    return jax.shard_map(
        local,
        mesh=mesh,
        in_specs=(
            P("doc", "feat", None),
            P("doc", "feat"),
            P("doc", "feat"),
            P("doc", "feat"),
            P(),
            P("doc", "feat", None),
            P("doc", "feat"),
            P("doc", "feat"),
            P("doc", "feat"),
            P(),
            P(),
        ),
        out_specs=P(("doc", "feat"), None),
        check_vma=False,
    )
```

profile of v0, /device:TPU:1, one launch (start us, length us, event | category | flops | bytes accessed | tf_op | source)
XLA Modules:
  0.0 622.7 jit_solution(13340459511408527445)
XLA Ops:
  0.0 1.4 fusion.58
  3.3 0.7 add_multiply_fusion
  4.0 18.3 %fusion.21 = f32[192,128,256]{1,2,0:T(8,128)} fusion(bf16[192,128,128]{2,1,0:T(8,128)(2,1)} %param.11, s32[]{:T(128)} %bitcast.13, s32[192]{0:T(256)S(1)} %bitcast.49), kind=kOutput, calls=%fused_computation.27 | convolution fusion | flops 1723858944 | bytes 31458052 | tf_op jit(solution)/shard_map/tij,tjk->tik/dot_general | solution.py:61
  22.3 24.8 %copy.21 = f32[192,128,256]{2,0,1:T(8,128)} copy(f32[192,128,256]{1,2,0:T(8,128)} %fusion.21) | data formatting | bytes 50331648 | tf_op jit(solution)/shard_map/tij,tjk->tik/dot_general | solution.py:61
  47.9 13.5 %fusion.38 = f32[12,128,256]{2,0,1:T(8,128)} fusion(f32[192,128,256]{2,0,1:T(8,128)} %copy.21, s32[192]{0:T(256)S(1)} %bitcast.48, pred[192]{0:T(512)(128)(4,1)S(1)} %iota_compare_fusion.3), kind=kOutput, calls=%fused_computation.46 | convolution fusion | flops 905974272 | bytes 26739648 | tf_op jit(solution)/shard_map/rt,tik->rik/dot_general | solution.py:66
  61.4 43.2 %all-reduce.1 = bf16[12,128,256]{2,0,1:T(8,128)(2,1)S(1)} all-reduce(f32[12,128,256]{2,0,1:T(8,128)} %fusion.38), channel_id=1, replica_groups=mesh['doc'=64,'feat'=4] {'feat'}, use_global_device_ids=true, to_apply=%region_3.4 | all-reduce | flops 393216 | bytes 2359296 | tf_op jit(solution)/shard_map/psum | solution.py:72
  104.7 0.2 constant_dynamic-slice_fusion
  104.9 5.5 collective-permute-start
  111.2 0.1 reduce_window_sum.11
  111.3 0.2 select_reduce_fusion
  111.5 0.8 scatter_custom_fusion
  112.3 0.7 all_to_all.9
  113.0 10.7 %all-to-all-start = ((s32[64,1,2]{2,1,0:T(1,128)}), s32[64,1,2]{2,1,0:T(1,128)S(1)}, u32[]{:S(2)}, u32[]{:S(2)}) async-start(s32[64,1,2]{2,1,0:T(1,128)} %bitcast.5), calls=%async_computation | async-start | bytes 65536 | tf_op jit(solution)/shard_map/all_to_all | solution.py:112
  123.8 0.6 dynamic_slice.12
  125.7 0.5 pad_maximum_fusion
  126.2 0.3 copy.22
  126.5 1.5 gather_fusion
  128.0 1.3 broadcast_select_fusion
  129.3 2.8 gather_fusion.1
  132.2 6.8 %fusion.27 = f32[64,128,256]{1,2,0:T(8,128)} fusion(bf16[64,128,128]{2,1,0:T(8,128)(2,1)S(1)} %copy-done, bf16[64,128,256]{2,1,0:T(8,128)(2,1)} %gather_fusion.1, pred[64]{0:T(512)(128)(4,1)S(1)} %and_bitcast_fusion), kind=kOutput, calls=%fused_computation.31 | convolution fusion | flops 538968064 | bytes 14680128 | tf_op jit(solution)/shard_map/tij,tik->tjk/dot_general | solution.py:98
  138.9 9.0 %copy.24 = f32[64,128,256]{2,1,0:T(8,128)} copy(f32[64,128,256]{1,2,0:T(8,128)} %fusion.27) | data formatting | bytes 16777216 | tf_op jit(solution)/shard_map/tij,tik->tjk/dot_general | solution.py:98
  147.9 7.8 %broadcast_in_dim.48 = f32[128,128,256]{2,1,0:T(8,128)} broadcast(f32[]{:T(128)} %constant.99.clone.1), dimensions={} | broadcast | bytes 16777220 | tf_op jit(solution)/shard_map/broadcast_in_dim | solution.py:100
  155.8 16.0 %scatter_fusion = f32[128,128,256]{2,1,0:T(8,128)} fusion(f32[128,128,256]{2,1,0:T(8,128)} %broadcast_in_dim.48, s32[64]{0:T(128)S(1)} %fusion.44, f32[64,128,256]{2,1,0:T(8,128)} %copy.24), kind=kCustom, calls=%fused_computation.3 | custom fusion | bytes 25166080 | tf_op jit(solution)/shard_map/scatter | solution.py:102
  171.8 28.5 %copy.25 = f32[64,2,128,256]{3,1,2,0:T(2,128)} copy(f32[64,2,128,256]{3,2,1,0:T(8,128)} %bitcast.47) | data formatting | bytes 33554432 | tf_op jit(solution)/shard_map/reshape | solution.py:106
  200.3 10.3 %all-to-all-start.1 = ((f32[64,2,128,256]{3,1,2,0:T(2,128)}), f32[64,2,128,256]{3,1,2,0:T(2,128)}, u32[]{:S(2)}, u32[]{:S(2)}) async-start(f32[64,2,128,256]{3,1,2,0:T(2,128)} %copy.25), calls=%async_computation.1 | async-start | bytes 33554432 | tf_op jit(solution)/shard_map/all_to_all | solution.py:105
  210.6 0.1 subtract_reduce_fusion
  210.7 0.1 sub.48
  210.8 365.2 %all-to-all-done.1 = f32[64,2,128,256]{3,1,2,0:T(2,128)} async-done(((f32[64,2,128,256]{3,1,2,0:T(2,128)}), f32[64,2,128,256]{3,1,2,0:T(2,128)}, u32[]{:S(2)}, u32[]{:S(2)}) %all-to-all-start.1) | async-done | bytes 16777248 | tf_op jit(solution)/shard_map/all_to_all | solution.py:105
  576.1 12.1 %copy.26 = f32[64,2,128,256]{3,1,0,2:T(2,128)} copy(f32[64,2,128,256]{3,1,2,0:T(2,128)} %all-to-all-done.1) | data formatting | bytes 33554432 | tf_op jit(solution)/shard_map/all_to_all | solution.py:105
  588.2 20.7 %reshape.87 = f32[128,128,256]{2,0,1:T(8,128)} reshape(f32[64,2,128,256]{3,1,0,2:T(2,128)} %copy.26) | data formatting | bytes 33554432 | tf_op jit(solution)/shard_map/reshape | solution.py:120
  608.9 9.4 %fusion.34 = f32[32,128,256]{2,0,1:T(8,128)S(1)} fusion(f32[128,128,256]{2,0,1:T(8,128)} %reshape.87, s32[128]{0:T(128)S(1)} %sub.48), kind=kOutput, calls=%fused_computation.43 | convolution fusion | flops 1610616832 | bytes 20972032 | tf_op jit(solution)/shard_map/bs,sjk->bjk/dot_general | solution.py:119
  618.3 4.4 copy.27
  (25 shorter events, 0.2 us)
Async XLA Ops:
  0.0 132.2 %copy-start = (bf16[64,128,128]{2,1,0:T(8,128)(2,1)S(1)}, bf16[64,128,128]{2,1,0:T(8,128)(2,1)}, u32[]{:S(2)}) copy-start(bf16[64,128,128]{2,1,0:T(8,128)(2,1)} %param.16) | copy-start | bytes 6291460
  22.3 25.6 %copy-start.2 = (s32[192,1]{0,1:T(1,128)S(1)}, s32[192,1]{0,1:T(1,128)}, u32[]{:S(2)}) copy-start(s32[192,1]{0,1:T(1,128)} %param.12) | copy-start | bytes 2308
  47.2 63.9 %copy-start.3 = (s32[64,1]{0,1:T(1,128)S(1)}, s32[64,1]{0,1:T(1,128)}, u32[]{:S(2)}) copy-start(s32[64,1]{0,1:T(1,128)} %param.18) | copy-start | bytes 772
  47.2 76.5 %copy-start.4 = (s32[64,1]{0,1:T(1,128)S(1)}, s32[64,1]{0,1:T(1,128)}, u32[]{:S(2)}) copy-start(s32[64,1]{0,1:T(1,128)} %param.17) | copy-start | bytes 772
  47.2 76.6 %copy-start.5 = (s32[65]{0:T(128)S(1)}, s32[65]{0:T(128)}, u32[]{:S(2)}) copy-start(s32[65]{0:T(128)} %param.20) | copy-start | bytes 784
  104.9 20.8 %collective-permute-start = (bf16[2,128,256]{2,0,1:T(2,128)(2,1)S(1)}, bf16[2,128,256]{2,0,1:T(2,128)(2,1)S(1)}, u32[]{:S(2)}, u32[]{:S(2)}) collective-permute-start(bf16[2,128,256]{2,0,1:T(2,128)(2,1)S(1)} %constant_dynamic-slice_fusion), channel_id=1, source_target_pairs={{0,4},{4,8},{8,12},{12,16},{16,20},{20,24},{24,28},{28,32},{32,36}... | collective-permute-start | bytes 393224 | tf_op jit(solution)/shard_map/ppermute | solution.py:18
  113.0 87.3 %all-to-all-start = ((s32[64,1,2]{2,1,0:T(1,128)}), s32[64,1,2]{2,1,0:T(1,128)S(1)}, u32[]{:S(2)}, u32[]{:S(2)}) async-start(s32[64,1,2]{2,1,0:T(1,128)} %bitcast.5), calls=%async_computation | async-start | bytes 65536 | tf_op jit(solution)/shard_map/all_to_all | solution.py:112
  200.3 375.8 %all-to-all-start.1 = ((f32[64,2,128,256]{3,1,2,0:T(2,128)}), f32[64,2,128,256]{3,1,2,0:T(2,128)}, u32[]{:S(2)}, u32[]{:S(2)}) async-start(f32[64,2,128,256]{3,1,2,0:T(2,128)} %copy.25), calls=%async_computation.1 | async-start | bytes 33554432 | tf_op jit(solution)/shard_map/all_to_all | solution.py:105
  588.2 34.5 %copy-start.1 = (bf16[64,128,128]{2,1,0:T(8,128)(2,1)S(1)}, bf16[64,128,128]{2,1,0:T(8,128)(2,1)}, u32[]{:S(2)}) copy-start(bf16[64,128,128]{2,1,0:T(8,128)(2,1)} %param.16) | copy-start | bytes 6291460
where the time goes:
time: 624 us; the launch traced here: 623 us
  waiting for transfers between devices  365 us (58%)
  local copies, waits for them, and re-layouts  132 us (21%)
  matrix products  48 us (8%)
  blocking collectives  43.2 us (7%)
  starting transfers between devices  26.6 us (4%)
    all_to_all x1, waiting for transfers between devices, local(): lax.all_to_all(outbox.reshape(doc_count, capacity, TILE, SKETCH), 'doc',...  365 us
    psum x1, blocking collectives, local(): own_rows = lax.psum(partial_value, 'feat').astype(jnp.bfloat16)  43.2 us
    reshape x1, local copies, waits for them, and re-layouts, local(): outbox.reshape(doc_count, capacity, TILE, SKETCH)  28.5 us
    dot_general x1, local copies, waits for them, and re-layouts, local(): jnp.einsum('tij,tjk->tik', b_tiles, panels, preferred_element_type=jnp.fl...  24.8 us
    reshape x1, local copies, waits for them, and re-layouts, local(): arrived_sums.reshape(-1, TILE, SKETCH)  20.7 us
    dot_general x1, matrix products, local(): jnp.einsum('tij,tjk->tik', b_tiles, panels, preferred_element_type=jnp.fl...  18.3 us
    scatter x1, local copies, waits for them, and re-layouts, local(): outbox = jnp.zeros((doc_count * capacity, TILE, SKETCH), jnp.float32).at[...  16 us
    dot_general x1, matrix products, local(): jnp.einsum('rt,tik->rik', chosen.astype(jnp.float32), tile_terms, precisi...  13.5 us
  transfers between devices with their start and end apart: 3, of which 1 were waited for; matrix products, arithmetic and copies ran while one was open for 12% of the time, Pallas kernels for 0%

commit v1 on v0

--- a/solution.py
+++ b/solution.py
@@ -69,7 +69,7 @@
     b_start = b_offsets[doc_here]
     b_length = b_offsets[doc_here + 1] - b_start
     shift_rows = a_offsets[doc_here] - b_start + MARGIN
-    own_rows = lax.psum(partial_value, "feat").astype(jnp.bfloat16)
+    own_rows = jnp.sum(lax.all_gather(partial_value, "feat"), axis=0).astype(jnp.bfloat16)
     last_rows = lax.dynamic_slice_in_dim(own_rows, b_length - MARGIN, MARGIN, 0)
     arrived = passed_along(last_rows, "doc", 1)
     source = jnp.concatenate([arrived, own_rows], axis=0)

time: 624 us -> 657 us (1.053)
  waiting for transfers between devices: 365 us -> 420 us
  blocking collectives: 43.2 us -> 0 us
  between operations: 4.73 us -> 18.3 us
    all_gather x0 -> x1, waiting for transfers between devices: none -> 52.6 us  [local(): lax.all_gather(partial_value, 'feat')]
    psum x1 -> x0, blocking collectives: 43.2 us -> none  [local(): own_rows = lax.psum(partial_value, 'feat').astype(jnp.bfloat16)]
  transfers between devices with their start and end apart: 3 -> 4, of which waited for: 1 -> 3; matrix products, arithmetic and copies ran while one was open for 12% -> 13% of each run, Pallas kernels for 0% -> 0%
where the time goes in v1:
time: 657 us; the launch traced here: 656 us
  waiting for transfers between devices  420 us (64%)
  local copies, waits for them, and re-layouts  134 us (20%)
  matrix products  47.3 us (7%)
  starting transfers between devices  29.5 us (4%)
  between operations  18.3 us (3%)
  other arithmetic  6.88 us (1%)
    all_to_all x1, waiting for transfers between devices, local(): lax.all_to_all(outbox.reshape(doc_count, capacity, TILE, SKETCH), 'doc',...  365 us
    all_gather x1, waiting for transfers between devices, local(): lax.all_gather(partial_value, 'feat')  52.6 us
    reshape x1, local copies, waits for them, and re-layouts, local(): outbox.reshape(doc_count, capacity, TILE, SKETCH)  28.5 us
    dot_general x1, local copies, waits for them, and re-layouts, local(): jnp.einsum('tij,tjk->tik', b_tiles, panels, preferred_element_type=jnp.fl...  24.9 us
    reshape x1, local copies, waits for them, and re-layouts, local(): arrived_sums.reshape(-1, TILE, SKETCH)  20.7 us
    dot_general x1, matrix products, local(): jnp.einsum('tij,tjk->tik', b_tiles, panels, preferred_element_type=jnp.fl...  18.3 us
    scatter x1, local copies, waits for them, and re-layouts, local(): outbox = jnp.zeros((doc_count * capacity, TILE, SKETCH), jnp.float32).at[...  16.1 us
  transfers between devices with their start and end apart: 4, of which 3 were waited for; matrix products, arithmetic and copies ran while one was open for 13% of the time, Pallas kernels for 0%

profile of v1, /device:TPU:1, one launch (start us, length us, event | category | flops | bytes accessed | tf_op | source)
XLA Modules:
  0.0 655.7 jit_solution(7076331839579209409)
XLA Ops:
  7.3 0.7 add_multiply_fusion
  8.0 18.3 %fusion.21 = f32[192,128,256]{1,2,0:T(8,128)} fusion(bf16[192,128,128]{2,1,0:T(8,128)(2,1)} %param.11, s32[]{:T(128)} %bitcast.13, s32[192]{0:T(256)S(1)} %bitcast.51), kind=kOutput, calls=%fused_computation.27 | convolution fusion | flops 1723858944 | bytes 31458052 | tf_op jit(solution)/shard_map/tij,tjk->tik/dot_general | solution.py:61
  26.3 24.9 %copy.20 = f32[192,128,256]{2,0,1:T(8,128)} copy(f32[192,128,256]{1,2,0:T(8,128)} %fusion.21) | data formatting | bytes 50331648 | tf_op jit(solution)/shard_map/tij,tjk->tik/dot_general | solution.py:61
  52.0 12.8 %fusion.38 = f32[12,128,256]{2,0,1:T(8,128)S(1)} fusion(f32[192,128,256]{2,0,1:T(8,128)} %copy.20, s32[192]{0:T(256)S(1)} %bitcast.50, pred[192]{0:T(512)(128)(4,1)S(1)} %iota_compare_fusion.3), kind=kOutput, calls=%fused_computation.46 | convolution fusion | flops 905974272 | bytes 26739648 | tf_op jit(solution)/shard_map/rt,tik->rik/dot_general | solution.py:66
  64.8 2.1 copy.21
  67.7 0.1 reduce_window_sum.11
  67.7 0.2 select_reduce_fusion
  68.0 0.8 scatter_custom_fusion
  68.7 0.7 all_to_all.9
  69.5 13.0 %all-to-all-start = ((s32[64,1,2]{2,1,0:T(1,128)}), s32[64,1,2]{2,1,0:T(1,128)S(1)}, u32[]{:S(2)}, u32[]{:S(2)}) async-start(s32[64,1,2]{2,1,0:T(1,128)} %bitcast.5), calls=%async_computation | async-start | bytes 65536 | tf_op jit(solution)/shard_map/all_to_all | solution.py:112
  82.5 0.7 fusion.58
  84.4 0.6 dynamic_slice.12
  86.3 52.6 %all-gather.3.cloned.1.call-done = f32[48,128,256]{2,1,0:T(8,128)} async-done(((f32[12,128,256]{2,1,0:T(8,128)}), f32[48,128,256]{2,1,0:T(8,128)}) %all-gather.3.cloned.1.call-update) | async-done | bytes 6291472 | tf_op jit(solution)/shard_map/all_gather | solution.py:72
  138.9 3.4 reduce_sum.22
  142.3 3.9 collective-permute-start
  146.2 1.9 collective-permute-done
  148.1 1.0 pad_maximum_fusion
  149.1 2.7 gather_fusion
  151.8 1.3 broadcast_select_fusion
  153.1 2.8 gather_fusion.1
  155.9 6.8 %fusion.27 = f32[64,128,256]{1,2,0:T(8,128)} fusion(bf16[64,128,128]{2,1,0:T(8,128)(2,1)S(1)} %copy-done, bf16[64,128,256]{2,1,0:T(8,128)(2,1)} %gather_fusion.1, pred[64]{0:T(512)(128)(4,1)S(1)} %and_bitcast_fusion), kind=kOutput, calls=%fused_computation.31 | convolution fusion | flops 538968064 | bytes 14680128 | tf_op jit(solution)/shard_map/tij,tik->tjk/dot_general | solution.py:98
  162.7 9.0 %copy.23 = f32[64,128,256]{2,1,0:T(8,128)} copy(f32[64,128,256]{1,2,0:T(8,128)} %fusion.27) | data formatting | bytes 16777216 | tf_op jit(solution)/shard_map/tij,tik->tjk/dot_general | solution.py:98
  171.7 7.8 %broadcast_in_dim.48 = f32[128,128,256]{2,1,0:T(8,128)} broadcast(f32[]{:T(128)} %constant.100.clone.1), dimensions={} | broadcast | bytes 16777220 | tf_op jit(solution)/shard_map/broadcast_in_dim | solution.py:100
  179.5 16.1 %scatter_fusion = f32[128,128,256]{2,1,0:T(8,128)} fusion(f32[128,128,256]{2,1,0:T(8,128)} %broadcast_in_dim.48, s32[64]{0:T(128)S(1)} %fusion.44, f32[64,128,256]{2,1,0:T(8,128)} %copy.23), kind=kCustom, calls=%fused_computation.3 | custom fusion | bytes 25166080 | tf_op jit(solution)/shard_map/scatter | solution.py:102
  195.6 28.5 %copy.24 = f32[64,2,128,256]{3,1,2,0:T(2,128)} copy(f32[64,2,128,256]{3,2,1,0:T(8,128)} %bitcast.48) | data formatting | bytes 33554432 | tf_op jit(solution)/shard_map/reshape | solution.py:106
  224.1 12.6 %all-to-all-start.1 = ((f32[64,2,128,256]{3,1,2,0:T(2,128)}), f32[64,2,128,256]{3,1,2,0:T(2,128)}, u32[]{:S(2)}, u32[]{:S(2)}) async-start(f32[64,2,128,256]{3,1,2,0:T(2,128)} %copy.24), calls=%async_computation.1 | async-start | bytes 33554432 | tf_op jit(solution)/shard_map/all_to_all | solution.py:105
  236.8 0.1 sub.48
  236.9 365.2 %all-to-all-done.1 = f32[64,2,128,256]{3,1,2,0:T(2,128)} async-done(((f32[64,2,128,256]{3,1,2,0:T(2,128)}), f32[64,2,128,256]{3,1,2,0:T(2,128)}, u32[]{:S(2)}, u32[]{:S(2)}) %all-to-all-start.1) | async-done | bytes 16777248 | tf_op jit(solution)/shard_map/all_to_all | solution.py:105
  602.2 12.1 %copy.25 = f32[64,2,128,256]{3,1,0,2:T(2,128)} copy(f32[64,2,128,256]{3,1,2,0:T(2,128)} %all-to-all-done.1) | data formatting | bytes 33554432 | tf_op jit(solution)/shard_map/all_to_all | solution.py:105
  614.3 20.7 %reshape.87 = f32[128,128,256]{2,0,1:T(8,128)} reshape(f32[64,2,128,256]{3,1,0,2:T(2,128)} %copy.25) | data formatting | bytes 33554432 | tf_op jit(solution)/shard_map/reshape | solution.py:120
  635.0 9.4 %fusion.34 = f32[32,128,256]{2,0,1:T(8,128)S(1)} fusion(f32[128,128,256]{2,0,1:T(8,128)} %reshape.87, s32[128]{0:T(128)S(1)} %sub.48), kind=kOutput, calls=%fused_computation.43 | convolution fusion | flops 1610616832 | bytes 20972032 | tf_op jit(solution)/shard_map/bs,sjk->bjk/dot_general | solution.py:119
  644.4 4.4 copy.26
  (30 shorter events, 0.3 us)
Async XLA Ops:
  6.5 149.4 %copy-start = (bf16[64,128,128]{2,1,0:T(8,128)(2,1)S(1)}, bf16[64,128,128]{2,1,0:T(8,128)(2,1)}, u32[]{:S(2)}) copy-start(bf16[64,128,128]{2,1,0:T(8,128)(2,1)} %param.16) | copy-start | bytes 6291460
  6.5 132.3 %all-gather.3.cloned.1.call-start = ((), (), s32[]{:S(2)}) async-start(), calls=%async_computation.2 | async-start | bytes 7864320 | tf_op jit(solution)/shard_map/all_gather | solution.py:72
  26.3 25.6 %copy-start.3 = (s32[192,1]{0,1:T(1,128)S(1)}, s32[192,1]{0,1:T(1,128)}, u32[]{:S(2)}) copy-start(s32[192,1]{0,1:T(1,128)} %param.12) | copy-start | bytes 2308
  51.2 16.3 %copy-start.4 = (s32[64,1]{0,1:T(1,128)S(1)}, s32[64,1]{0,1:T(1,128)}, u32[]{:S(2)}) copy-start(s32[64,1]{0,1:T(1,128)} %param.18) | copy-start | bytes 772
  51.2 31.3 %copy-start.2 = (s32[65]{0:T(128)S(1)}, s32[65]{0:T(128)}, u32[]{:S(2)}) copy-start(s32[65]{0:T(128)} %param.15) | copy-start | bytes 784
  51.2 33.2 %copy-start.5 = (s32[65]{0:T(128)S(1)}, s32[65]{0:T(128)}, u32[]{:S(2)}) copy-start(s32[65]{0:T(128)} %param.20) | copy-start | bytes 784
  51.2 35.0 %copy-start.6 = (s32[64,1]{0,1:T(1,128)S(1)}, s32[64,1]{0,1:T(1,128)}, u32[]{:S(2)}) copy-start(s32[64,1]{0,1:T(1,128)} %param.17) | copy-start | bytes 772
  69.5 154.6 %all-to-all-start = ((s32[64,1,2]{2,1,0:T(1,128)}), s32[64,1,2]{2,1,0:T(1,128)S(1)}, u32[]{:S(2)}, u32[]{:S(2)}) async-start(s32[64,1,2]{2,1,0:T(1,128)} %bitcast.5), calls=%async_computation | async-start | bytes 65536 | tf_op jit(solution)/shard_map/all_to_all | solution.py:112
  142.3 5.8 collective-permute-start
  224.1 378.1 %all-to-all-start.1 = ((f32[64,2,128,256]{3,1,2,0:T(2,128)}), f32[64,2,128,256]{3,1,2,0:T(2,128)}, u32[]{:S(2)}, u32[]{:S(2)}) async-start(f32[64,2,128,256]{3,1,2,0:T(2,128)} %copy.24), calls=%async_computation.1 | async-start | bytes 33554432 | tf_op jit(solution)/shard_map/all_to_all | solution.py:105
  614.3 34.5 %copy-start.1 = (bf16[64,128,128]{2,1,0:T(8,128)(2,1)S(1)}, bf16[64,128,128]{2,1,0:T(8,128)(2,1)}, u32[]{:S(2)}) copy-start(bf16[64,128,128]{2,1,0:T(8,128)(2,1)} %param.16) | copy-start | bytes 6291460
Sparse Core Ops, SparseCore 0:
  67.0 71.8 all-gather.2
